TPU v7x, 128 devices: a whole 4x4x4 slice. The times are simulated.
128 devices in a mesh: row: 8 (over z, core), col: 16 (over x, y).
Axes of the slice: x: 4, y: 4, z: 4, core: 2. Of those that a mesh axis runs over, the one named last changes fastest.
Arguments:
- velocity: float32 [2, 512, 128, 384], P(None, 'col', 'row'), may hold values from -6 to 6
- synthesis: float32 [384, 384], replicated
- analysis: float32 [384, 384], replicated
- radial_eigen: float32 [384], replicated, may hold values from 0.05 to 4
- pair_list: int32 [256, 2], replicated, may hold values from 0 to 511, as said below
- owner_slot: int32 [256], replicated, may hold values from 0 to 255, each once
- freq_list: int32 [4], replicated, may hold values from 0 to 255
- snap_index: int32 [1], replicated, may hold values from 0 to 254
- block_dft: float32 [256, 4, 2, 384], P(('row', 'col')), may hold values from -6 to 6
- spectra: float32 [256, 4, 2, 384, 384], P(('row', 'col')), may hold values from -6 to 6
Outputs:
- velocity_next: float32 [2, 512, 128, 384], P(None, 'col', 'row')
- block_sums: float32 [256, 4, 2, 384], P(('row', 'col'))
- spectra_next: float32 [256, 4, 2, 384, 384], P(('row', 'col'))
Inputs may be any that keep to these rules, and one draw needn't show every extreme that they name: `pair_list`: the pairs are distinct; the axial index is below 128 and the wavenumber below 512. Of the devices of the solver layout (row index times the size of col plus col index, holding axial indices row * 16 onward and wavenumbers col * 512 / size of col onward), each holds at most 8 selected pairs and some hold exactly 8. `owner_slot`: each slot once.
All inputs are finite; a program needn't handle non-finite values.
Results may differ from a plain program's by a relative error of at most 0.0001.
Values sent between devices are 32-bit elements; how exact they have to be, the bound alone decides.
No kernel may reach another device: no remote copies, remote signals or barrier semaphores. Data moves between devices by JAX's collectives and lax.ppermute only.
A program may use at most 128 MiB of HBM per device.

v0:
```python
import math
import jax
import jax.numpy as jnp
from jax import lax
from jax.sharding import PartitionSpec as P

NBLK = 256
HOLD = 8
viscosity = 4e-06
axial_scale = 2.0
nonlinear_gain = 0.1
highest = lax.Precision.HIGHEST


def sent_together(arrays, axis, split_dim, concat_dim, along):
    both = jnp.concatenate(arrays, axis=along)
    whole, at, outs = (
        lax.all_to_all(both, axis, split_axis=split_dim, concat_axis=concat_dim, tiled=True),
        0,
        [],
    )
    for a in arrays:
        outs.append(lax.slice_in_dim(whole, at, at + a.shape[along], axis=along))
        at += a.shape[along]
    return tuple(outs)


def circle_tables(mode_count, point_count):
    mode_ids = jnp.arange(mode_count, dtype=jnp.int32)[:, None]
    point_ids = jnp.arange(point_count, dtype=jnp.int32)[None, :]
    angle = (mode_ids * point_ids % point_count).astype(jnp.float32) * (2.0 * math.pi / point_count)
    cosine = jnp.cos(angle)
    sine = jnp.sin(angle)
    weight = jnp.where(mode_ids == 0, 1.0, 2.0) * mode_count ** (-0.5)
    keeping = jnp.where(mode_ids == 0, 0.0, math.sqrt(mode_count) / point_count)
    synth_table = jnp.concatenate([weight * cosine, -weight * sine], axis=0)
    anal_table = jnp.concatenate([keeping * cosine, -keeping * sine], axis=0)
    return (synth_table, anal_table)


def circle_forcing(moved, synth_table, anal_table):
    columns = moved.reshape(synth_table.shape[0], -1)
    physical = lax.dot_general(synth_table, columns, (((0,), (0,)), ((), ())), precision=highest)
    squared = physical * physical
    return jnp.dot(anal_table, squared, precision=highest).reshape(moved.shape)


def damping_for(axial_int, mode_int, radial_eigen):
    axial_ids = axial_int.astype(jnp.float32) * axial_scale
    mode_ids = mode_int.astype(jnp.float32)
    return 1.0 / (
        1.0
        + viscosity * (axial_ids[None, :, None] ** 2 + mode_ids[:, None, None] ** 2)
        + radial_eigen[None, None, :]
    )


def radial_apply(rhs, analysis, synthesis, damping):
    radial_pts = rhs.shape[-1]
    coeffs = (
        jnp.dot(rhs.reshape(-1, radial_pts), analysis, precision=highest).reshape(rhs.shape)
        * damping[None]
    )
    return jnp.dot(coeffs.reshape(-1, radial_pts), synthesis, precision=highest).reshape(rhs.shape)


def window_terms(freq_list, snap_now):
    position = snap_now.astype(jnp.float32)
    window = 0.54 - 0.46 * jnp.cos(2.0 * math.pi * position / NBLK)
    phase = (freq_list * snap_now % NBLK).astype(jnp.float32) * (2.0 * math.pi / NBLK)
    return (window * jnp.cos(phase), -window * jnp.sin(phase))


def add_snapshot(block, snapshot, real_w, imag_w):
    real_new = (
        block[:, :, 0]
        + real_w[None, :, None] * snapshot[0][:, None, :]
        - imag_w[None, :, None] * snapshot[1][:, None, :]
    )
    imag_new = (
        block[:, :, 1]
        + real_w[None, :, None] * snapshot[1][:, None, :]
        + imag_w[None, :, None] * snapshot[0][:, None, :]
    )
    return jnp.stack([real_new, imag_new], axis=2)


def spectral_update(spectrum_one, old_block, new_block):
    old_real, old_imag = (old_block[:, 0], old_block[:, 1])
    new_real, new_imag = (new_block[:, 0], new_block[:, 1])
    left_real = jnp.stack([new_real, new_imag, old_real, old_imag], axis=1)
    left_imag = jnp.stack([new_imag, -new_real, old_imag, -old_real], axis=1)
    left = jnp.stack([left_real, left_imag], axis=1)
    right = jnp.stack([new_real, new_imag, -old_real, -old_imag], axis=1)
    return spectrum_one + jnp.einsum("fckr,fkq->fcrq", left, right, precision=highest)


def local(
    velocity,
    synthesis,
    analysis,
    radial_eigen,
    pair_list,
    owner_slot,
    freq_list,
    snap_index,
    block_dft,
    spectra,
):
    modes_dev = velocity.shape[1]
    axial_dev = velocity.shape[2]
    col_count = lax.axis_size("col")
    modes_all = modes_dev * col_count
    synth_table, anal_table = circle_tables(modes_all, 3 * modes_all)
    row_index = lax.axis_index("row")
    col_index = lax.axis_index("col")
    axial_int = row_index * axial_dev + jnp.arange(axial_dev, dtype=jnp.int32)
    mode_int = col_index * modes_dev + jnp.arange(modes_dev, dtype=jnp.int32)
    share = axial_dev // col_count
    state = lax.all_to_all(velocity, "col", split_axis=2, concat_axis=1, tiled=True)
    local_axial = row_index * axial_dev + col_index * share + jnp.arange(share, dtype=jnp.int32)
    local_damping = damping_for(local_axial, jnp.arange(modes_all, dtype=jnp.int32), radial_eigen)
    stepped = []
    for section_index in range(2):
        rhs = state - nonlinear_gain * circle_forcing(state, synth_table, anal_table)
        state = radial_apply(rhs, analysis, synthesis, local_damping)
        stepped.append(state)
    first, second = sent_together((stepped[0], stepped[1]), "col", 1, 2, 0)
    snapshots = [first, second]
    current = snapshots[1]
    selected = pair_list.shape[0]
    slot_ids = jnp.arange(selected, dtype=jnp.int32)
    pair_of_slot = jnp.zeros((selected,), jnp.int32).at[owner_slot].set(slot_ids)
    axial_sel = pair_list[pair_of_slot, 0]
    mode_sel = pair_list[pair_of_slot, 1]
    holder = axial_sel // axial_dev * col_count + mode_sel // modes_dev
    my_index = row_index * col_count + col_index
    both_snaps = jnp.stack(snapshots, axis=0)
    picked = both_snaps[:, :, mode_sel % modes_dev, axial_sel % axial_dev, :]
    slots_here = block_dft.shape[0]
    same_holder = holder[:, None] == holder[None, :]
    earlier = slot_ids[:, None] > slot_ids[None, :]
    position = jnp.sum(jnp.where(same_holder & earlier, 1, 0), axis=1).astype(jnp.int32)
    held_mask = holder == my_index
    hold_slots = HOLD
    placing = jnp.where(
        held_mask[None, :]
        & (position[None, :] == jnp.arange(hold_slots, dtype=jnp.int32)[:, None]),
        1.0,
        0.0,
    )
    compact = jnp.einsum("ps,abst->abpt", placing, picked, precision=highest)
    gathered = lax.all_gather(compact, ("row", "col"), axis=2, tiled=True)
    wanted = my_index * slots_here + jnp.arange(slots_here, dtype=jnp.int32)
    source = holder[wanted] * hold_slots + position[wanted]
    mine = jnp.take(gathered, source, axis=2)
    block = block_dft
    for section_index in range(2):
        real_w, imag_w = window_terms(freq_list, snap_index[0] + section_index)
        block = add_snapshot(block, mine[section_index], real_w, imag_w)
    spectra_next = jax.vmap(spectral_update)(spectra, block_dft, block)
    return (current, block, spectra_next)


def solution(mesh):
    return jax.shard_map(
        local,
        mesh=mesh,
        in_specs=(
            P(None, "col", "row", None),
            P(),
            P(),
            P(),
            P(),
            P(),
            P(),
            P(),
            P(("row", "col"), None, None, None),
            P(("row", "col"), None, None, None, None),
        ),
        out_specs=(
            P(None, "col", "row", None),
            P(("row", "col"), None, None, None),
            P(("row", "col"), None, None, None, None),
        ),
        check_vma=False,
    )
```

profile of v0, /device:TPU:1, one launch (start us, length us, event | category | flops | bytes accessed | tf_op | source)
XLA Modules:
  0.0 276.6 jit_solution(14870041637013253507)
XLA Ops:
  7.2 3.1 %copy.47 = f32[2,32,16,384]{3,1,0,2:T(8,128)} copy(f32[2,32,16,384]{3,2,1,0:T(8,128)} %param.10) | data formatting | bytes 3145728 | tf_op args[0]
  10.3 7.6 %all-to-all-start = ((f32[2,32,16,384]{3,1,0,2:T(8,128)}), f32[2,32,16,384]{3,1,0,2:T(8,128)S(1)}, u32[]{:S(2)}, u32[]{:S(2)}) async-start(f32[2,32,16,384]{3,1,0,2:T(8,128)} %copy.47), calls=%async_computation | async-start | bytes 3145728 | tf_op jit(solution)/shard_map/all_to_all | solution.py:120
  18.2 14.2 %fusion.12 = (f32[512,1536]{1,0:T(8,128)}, f32[512,1536]{1,0:T(8,128)}) fusion(f32[512]{0:T(512)S(1)} %select_multiply_fusion, f32[512]{0:T(512)S(1)} %fusion.55), kind=kLoop, calls=%fused_computation.27 | loop fusion | flops 8650752 | bytes 6295552 | tf_op jit(solution)/shard_map/mul | solution.py:36
  32.4 14.7 %fusion.13 = (f32[512,1536]{1,0:T(8,128)}, f32[512,1536]{1,0:T(8,128)}) fusion(f32[512]{0:T(512)S(1)} %fusion.43, f32[512]{0:T(512)S(1)} %fusion.54), kind=kLoop, calls=%fused_computation.28 | loop fusion | flops 8650752 | bytes 6295552 | tf_op jit(solution)/shard_map/mul | solution.py:37
  49.0 12.0 %fusion.4 = f32[1536,384]{1,0:T(8,128)S(1)} fusion(f32[1024,384]{1,0:T(8,128)S(1)} %bitcast.85, f32[512,1536]{1,0:T(8,128)} %get-tuple-element.48, f32[512,1536]{1,0:T(8,128)S(1)} %copy-done.6), kind=kOutput, calls=%fused_computation.15 | convolution fusion | flops 7249920000 | bytes 10223616 | tf_op jit(solution)/shard_map/dot_general | solution.py:43
  61.0 10.1 %multiply_subtract_fusion.1 = f32[1024,384]{1,0:T(8,128)S(1)} fusion(f32[1024,384]{1,0:T(8,128)S(1)} %bitcast.86, f32[1536,384]{1,0:T(8,128)S(1)} %fusion.4, f32[512,1536]{1,0:T(8,128)S(1)} %copy-done.4, f32[512,1536]{1,0:T(8,128)S(1)} %copy-done.3), kind=kOutput, calls=%fused_computation.38 | convolution fusion | flops 7250116608 | bytes 11796480 | tf_op jit(solution)/shard_map/dot_general | solution.py:45
  71.2 3.2 %convolution_multiply_fusion = f32[2,512,384]{2,1,0:T(8,128)S(1)} fusion(f32[2,512,384]{2,1,0:T(8,128)S(1)} %bitcast.87, f32[512,384]{1,0:T(8,128)S(1)} %add_divide_fusion, f32[384,384]{1,0:T(8,128)S(1)} %copy-done), kind=kOutput, calls=%fused_computation.40 | convolution fusion | flops 1812332544 | bytes 4521984 | tf_op jit(solution)/shard_map/dot_general | solution.py:61
  74.4 3.2 %fusion.77 = f32[1024,384]{1,0:T(8,128)S(1)} fusion(f32[1024,384]{1,0:T(8,128)S(1)} %bitcast.83, f32[384,384]{1,0:T(8,128)S(1)} %copy-done.8), kind=kOutput, calls=%fused_computation.149 | convolution fusion | flops 1811939328 | bytes 3735552 | tf_op jit(solution)/shard_map/dot_general | solution.py:64
  77.6 10.0 %fusion.5 = f32[1536,384]{1,0:T(8,128)S(1)} fusion(f32[1024,384]{1,0:T(8,128)S(1)} %fusion.77, f32[512,1536]{1,0:T(8,128)S(1)} %copy-done.7, f32[512,1536]{1,0:T(8,128)S(1)} %copy-done.6), kind=kOutput, calls=%fused_computation.16 | convolution fusion | flops 7249920000 | bytes 10223616 | tf_op jit(solution)/shard_map/dot_general | solution.py:43
  87.6 10.4 %multiply_subtract_fusion = f32[1024,384]{1,0:T(8,128)S(1)} fusion(f32[1024,384]{1,0:T(8,128)S(1)} %fusion.77, f32[1536,384]{1,0:T(8,128)S(1)} %fusion.5, f32[512,1536]{1,0:T(8,128)S(1)} %copy-done.4, f32[512,1536]{1,0:T(8,128)S(1)} %copy-done.3), kind=kOutput, calls=%fused_computation.37 | convolution fusion | flops 7250116608 | bytes 11796480 | tf_op jit(solution)/shard_map/dot_general | solution.py:45
  98.0 3.2 %fusion.29 = f32[2,512,384]{2,1,0:T(8,128)S(1)} fusion(f32[2,512,384]{2,1,0:T(8,128)S(1)} %bitcast.84, f32[384,384]{1,0:T(8,128)S(1)} %copy-done), kind=kOutput, calls=%fused_computation.47 | convolution fusion | flops 1811939328 | bytes 3735552 | tf_op jit(solution)/shard_map/dot_general | solution.py:61
  101.2 3.2 %fusion.21 = f32[2,512,1,384]{3,1,0,2:T(8,128)S(1)} fusion(f32[2,512,384]{2,1,0:T(8,128)S(1)} %fusion.29, f32[512,384]{1,0:T(8,128)S(1)} %add_divide_fusion, f32[384,384]{1,0:T(8,128)S(1)} %copy-done.8), kind=kOutput, calls=%fused_computation.39 | convolution fusion | flops 1812332544 | bytes 4521984 | tf_op jit(solution)/shard_map/dot_general | solution.py:64
  104.7 3.7 %copy.49 = f32[4,512,1,384]{3,0,2,1:T(4,128)} copy(f32[4,512,1,384]{3,1,0,2:T(8,128)S(1)} %pad_maximum_fusion.10) | data formatting | bytes 6291456 | tf_op jit(solution)/shard_map/concatenate | solution.py:16
  108.3 6.8 %all-to-all-start.1 = ((f32[4,512,1,384]{3,0,2,1:T(4,128)}), f32[4,512,1,384]{3,0,2,1:T(4,128)S(1)}, u32[]{:S(2)}, u32[]{:S(2)}) async-start(f32[4,512,1,384]{3,0,2,1:T(4,128)} %copy.49), calls=%async_computation.1 | async-start | bytes 6291456 | tf_op jit(solution)/shard_map/all_to_all | solution.py:18
  116.6 2.5 gather_fusion.1
  119.1 2.5 gather_fusion
  121.8 33.5 %all-to-all-done.1 = f32[4,512,1,384]{3,0,2,1:T(4,128)S(1)} async-done(((f32[4,512,1,384]{3,0,2,1:T(4,128)}), f32[4,512,1,384]{3,0,2,1:T(4,128)S(1)}, u32[]{:S(2)}, u32[]{:S(2)}) %all-to-all-start.1) | async-done | bytes 3145760 | tf_op jit(solution)/shard_map/all_to_all | solution.py:18
  156.2 2.9 %slice_bitcast_fusion = (f32[1,2,32,16,384]{4,1,3,2,0:T(2,128)S(1)}, f32[1,2,32,16,384]{4,1,3,2,0:T(2,128)S(1)}, f32[2,32,16,384]{3,0,2,1:T(2,128)}) fusion(f32[4,32,16,1,384]{4,0,2,1,3:T(4,128)S(1)} %bitcast.80), kind=kLoop, calls=%fused_computation.32 | loop fusion | bytes 7864320 | tf_op jit(solution)/shard_map/stack | solution.py:138
  160.8 3.7 %gather_fusion.4 = f32[256,2,2,384]{3,2,1,0:T(2,128)} fusion(f32[2,2,32,16,384]{4,1,3,2,0:T(2,128)S(1)} %pad_maximum_fusion.11, s32[256]{0:T(256)S(1)} %bitcast.77), kind=kCustom, calls=%fused_computation.4 | custom fusion | bytes 3147776 | tf_op jit(solution)/shard_map/gather | solution.py:139
  164.5 3.1 %fusion.24 = f32[2,2,8,384]{3,2,1,0:T(8,128)} fusion(f32[2,2,256,384]{3,1,0,2:T(2,128)} %bitcast.82, s32[256]{0:T(256)S(1)} %select_reduce_fusion, pred[256]{0:T(512)(128)(4,1)S(1)} %get-tuple-element.24), kind=kOutput, calls=%fused_computation.43 | convolution fusion | flops 37754880 | bytes 1623296 | tf_op jit(solution)/shard_map/ps,abst->abpt/dot_general | solution.py:152
  171.2 69.5 %all-gather.2.cloned.1.call-done = f32[2,2,1024,384]{3,2,1,0:T(8,128)} async-done(((f32[2,2,8,384]{3,2,1,0:T(8,128)}), f32[2,2,1024,384]{3,2,1,0:T(8,128)}) %all-gather.2.cloned.1.call-update) | async-done | bytes 6291472 | tf_op jit(solution)/shard_map/all_gather | solution.py:153
  240.7 10.5 %copy.54 = f32[2,2,1024,384]{3,1,2,0:T(2,128)} copy(f32[2,2,1024,384]{3,2,1,0:T(8,128)} %all-gather.2.cloned.1.call-done) | data formatting | bytes 12582912 | tf_op jit(solution)/shard_map/all_gather | solution.py:153
  251.3 3.4 %gather_fusion.5 = f32[2,2,2,384]{3,2,1,0:T(2,128)S(1)} fusion(f32[2,2,1024,384]{3,1,2,0:T(2,128)} %copy.54, s32[1024]{0:T(1024)S(1)} %pad_clamp_fusion), kind=kCustom, calls=%fused_computation.5 | custom fusion | bytes 24584 | tf_op jit(solution)/shard_map/jit(_take)/gather | solution.py:156
  255.6 14.0 %convolution_add_fusion = f32[2,4,2,384,384]{4,3,2,1,0:T(8,128)} fusion(f32[2,4,2,384,384]{4,3,2,1,0:T(8,128)} %param.19, f32[2,4,2,4,384]{4,1,3,0,2:T(4,128)S(1)} %pad_maximum_fusion.16, f32[2,4,4,384,1]{3,1,2,0,4:T(4,128)S(1)} %get-tuple-element.30), kind=kOutput, calls=%fused_computation.14 | convolution fusion | flops 115605504 | bytes 19021824 | tf_op jit(solution)/shard_map/vmap(fckr,fkq->fcrq)/dot_general | solution.py:95
  (68 shorter events, 10.1 us)
Async XLA Ops:
  7.2 64.0 %copy-start = (f32[384,384]{1,0:T(8,128)S(1)}, f32[384,384]{1,0:T(8,128)}, u32[]{:S(2)}) copy-start(f32[384,384]{1,0:T(8,128)} %param.12) | copy-start | bytes 1769476
  7.2 10.8 %copy-start.10 = (f32[384]{0:T(512)S(1)}, f32[384]{0:T(512)}, u32[]{:S(2)}) copy-start(f32[384]{0:T(512)} %param.13) | copy-start | bytes 4612
  10.3 36.8 %all-to-all-start = ((f32[2,32,16,384]{3,1,0,2:T(8,128)}), f32[2,32,16,384]{3,1,0,2:T(8,128)S(1)}, u32[]{:S(2)}, u32[]{:S(2)}) async-start(f32[2,32,16,384]{3,1,0,2:T(8,128)} %copy.47), calls=%async_computation | async-start | bytes 3145728 | tf_op jit(solution)/shard_map/all_to_all | solution.py:120
  47.1 1.9 copy-start.6
  49.0 12.0 %copy-start.3 = (f32[512,1536]{1,0:T(8,128)S(1)}, f32[512,1536]{1,0:T(8,128)}, u32[]{:S(2)}) copy-start(f32[512,1536]{1,0:T(8,128)} %get-tuple-element.49) | copy-start | bytes 9437188
  49.0 12.0 %copy-start.4 = (f32[512,1536]{1,0:T(8,128)S(1)}, f32[512,1536]{1,0:T(8,128)}, u32[]{:S(2)}) copy-start(f32[512,1536]{1,0:T(8,128)} %get-tuple-element.50) | copy-start | bytes 9437188
  71.1 3.2 %copy-start.8 = (f32[384,384]{1,0:T(8,128)S(1)}, f32[384,384]{1,0:T(8,128)}, u32[]{:S(2)}) copy-start(f32[384,384]{1,0:T(8,128)} %param.11) | copy-start | bytes 1769476
  71.1 6.5 %copy-start.7 = (f32[512,1536]{1,0:T(8,128)S(1)}, f32[512,1536]{1,0:T(8,128)}, u32[]{:S(2)}) copy-start(f32[512,1536]{1,0:T(8,128)} %get-tuple-element.48) | copy-start | bytes 9437188
  108.3 6.8 %copy-start.11 = (s32[256]{0:T(256)S(1)}, s32[256]{0:T(256)}, u32[]{:S(2)}) copy-start(s32[256]{0:T(256)} %param.15) | copy-start | bytes 3076
  108.3 8.3 %copy-start.2 = (s32[256,2]{0,1:T(2,128)S(1)}, s32[256,2]{0,1:T(2,128)}, u32[]{:S(2)}) copy-start(s32[256,2]{0,1:T(2,128)} %param.14) | copy-start | bytes 6148
  108.3 47.0 %all-to-all-start.1 = ((f32[4,512,1,384]{3,0,2,1:T(4,128)}), f32[4,512,1,384]{3,0,2,1:T(4,128)S(1)}, u32[]{:S(2)}, u32[]{:S(2)}) async-start(f32[4,512,1,384]{3,0,2,1:T(4,128)} %copy.49), calls=%async_computation.1 | async-start | bytes 6291456 | tf_op jit(solution)/shard_map/all_to_all | solution.py:18
  115.1 125.6 %all-gather.2.cloned.1.call-start = ((), (), s32[]{:S(2)}) async-start(), calls=%async_computation.2 | async-start | bytes 6340608 | tf_op jit(solution)/shard_map/all_gather | solution.py:153
  160.8 9.0 %copy-start.9 = (f32[2,4,2,384]{3,2,1,0:T(2,128)S(1)}, f32[2,4,2,384]{3,2,1,0:T(2,128)}, u32[]{:S(2)}) copy-start(f32[2,4,2,384]{3,2,1,0:T(2,128)} %param.18) | copy-start | bytes 73732
  160.8 9.0 %copy-start.12 = (s32[4]{0:T(128)S(1)}, s32[4]{0:T(128)}, u32[]{:S(2)}) copy-start(s32[4]{0:T(128)} %param.16) | copy-start | bytes 52
  164.5 5.4 %copy-start.5 = (f32[2,32,16,384]{3,0,2,1:T(2,128)S(1)}, f32[2,32,16,384]{3,0,2,1:T(2,128)}, u32[]{:S(2)}) copy-start(f32[2,32,16,384]{3,0,2,1:T(2,128)} %get-tuple-element.28) | copy-start | bytes 4718596
  255.6 14.0 %copy-start.1 = (f32[384,384]{1,0:T(8,128)S(1)}, f32[384,384]{1,0:T(8,128)}, u32[]{:S(2)}) copy-start(f32[384,384]{1,0:T(8,128)} %param.12) | copy-start | bytes 1769476
Sparse Core Ops, SparseCore 0:
  167.8 72.9 all-gather.1
where the time goes:
time: 280 us; the launch traced here: 277 us
  waiting for transfers between devices  103 us (37%)
  matrix products  72.4 us (26%)
  local copies, waits for them, and re-layouts  39.7 us (14%)
  other arithmetic  31.6 us (11%)
  between operations  15.6 us (6%)
  starting transfers between devices  14.4 us (5%)
    all_gather x1, waiting for transfers between devices, local(): gathered = lax.all_gather(compact, ('row', 'col'), axis=2, tiled=True)  69.5 us
    all_to_all x1, waiting for transfers between devices, sent_together(): lax.all_to_all(both, axis, split_axis=split_dim, concat_axis=concat_dim,...  33.5 us
    dot_general x2, matrix products, circle_forcing(): lax.dot_general(synth_table, columns, (((0,), (0,)), ((), ())), precision...  22 us
    dot_general x2, matrix products, circle_forcing(): return jnp.dot(anal_table, squared, precision=highest).reshape(moved.shape)  20.5 us
    mul x1, other arithmetic, circle_tables(): anal_table = jnp.concatenate([keeping * cosine, -keeping * sine], axis=0)  14.7 us
    mul x1, other arithmetic, circle_tables(): synth_table = jnp.concatenate([weight * cosine, -weight * sine], axis=0)  14.2 us
    dot_general x1, matrix products, spectral_update(): jnp.einsum('fckr,fkq->fcrq', left, right, precision=highest)  14 us
    all_gather x1, local copies, waits for them, and re-layouts, local(): gathered = lax.all_gather(compact, ('row', 'col'), axis=2, tiled=True)  10.5 us
  transfers between devices with their start and end apart: 3, of which 2 were waited for; matrix products, arithmetic and copies ran while one was open for 14% of the time, Pallas kernels for 0%

commit v1 on v0

--- a/solution.py
+++ b/solution.py
@@ -10,6 +10,11 @@
 axial_scale = 2.0
 nonlinear_gain = 0.1
 highest = lax.Precision.HIGHEST
+
+
+def all_by_exchange(shard, name, d):
+    sent = jnp.stack([shard] * lax.axis_size(name))
+    return jnp.concatenate(lax.all_to_all(sent, name, 0, 0), axis=d)
 
 
 def sent_together(arrays, axis, split_dim, concat_dim, along):
@@ -150,7 +155,7 @@
         0.0,
     )
     compact = jnp.einsum("ps,abst->abpt", placing, picked, precision=highest)
-    gathered = lax.all_gather(compact, ("row", "col"), axis=2, tiled=True)
+    gathered = all_by_exchange(compact, ("row", "col"), 2)
     wanted = my_index * slots_here + jnp.arange(slots_here, dtype=jnp.int32)
     source = holder[wanted] * hold_slots + position[wanted]
     mine = jnp.take(gathered, source, axis=2)

time: 280 us -> 292 us (1.043)
  between operations: 15.6 us -> 2.38 us
  local copies, waits for them, and re-layouts: 39.7 us -> 51.6 us
  starting transfers between devices: 14.4 us -> 26 us
    all_to_all x0 -> x1, waiting for transfers between devices: none -> 71.6 us  [all_by_exchange(): return jnp.concatenate(lax.all_to_all(sent, name, 0, 0), axis=d)]
    all_gather x1 -> x0, waiting for transfers between devices: 69.5 us -> none  [local(): gathered = lax.all_gather(compact, ('row', 'col'), axis=2, tiled=True)]
    all_to_all x0 -> x1, starting transfers between devices: none -> 11.6 us  [all_by_exchange(): return jnp.concatenate(lax.all_to_all(sent, name, 0, 0), axis=d)]
    all_gather x1 -> x0, local copies, waits for them, and re-layouts: 10.5 us -> none  [local(): gathered = lax.all_gather(compact, ('row', 'col'), axis=2, tiled=True)]
    reshape x0 -> x1, local copies, waits for them, and re-layouts: none -> 10.3 us  [all_by_exchange(): return jnp.concatenate(lax.all_to_all(sent, name, 0, 0), axis=d)]
    all_to_all x0 -> x1, local copies, waits for them, and re-layouts: none -> 5.89 us  [all_by_exchange(): return jnp.concatenate(lax.all_to_all(sent, name, 0, 0), axis=d)]
    another operation x0 -> x1, local copies, waits for them, and re-layouts: none -> 3.51 us  [all_by_exchange(): sent = jnp.stack([shard] * lax.axis_size(name))]
  transfers between devices with their start and end apart: 3 -> 3, of which waited for: 2 -> 2; matrix products, arithmetic and copies ran while one was open for 14% -> 13% of each run, Pallas kernels for 0% -> 0%
where the time goes in v1:
time: 292 us; the launch traced here: 288 us
  waiting for transfers between devices  105 us (36%)
  matrix products  70.2 us (24%)
  local copies, waits for them, and re-layouts  51.6 us (18%)
  other arithmetic  32.8 us (11%)
  starting transfers between devices  26 us (9%)
    all_to_all x1, waiting for transfers between devices, all_by_exchange(): return jnp.concatenate(lax.all_to_all(sent, name, 0, 0), axis=d)  71.6 us
    all_to_all x1, waiting for transfers between devices, sent_together(): lax.all_to_all(both, axis, split_axis=split_dim, concat_axis=concat_dim,...  33.6 us
    dot_general x2, matrix products, circle_forcing(): lax.dot_general(synth_table, columns, (((0,), (0,)), ((), ())), precision...  22 us
    dot_general x2, matrix products, circle_forcing(): return jnp.dot(anal_table, squared, precision=highest).reshape(moved.shape)  20.2 us
    mul x1, other arithmetic, circle_tables(): anal_table = jnp.concatenate([keeping * cosine, -keeping * sine], axis=0)  14.3 us
    mul x1, other arithmetic, circle_tables(): synth_table = jnp.concatenate([weight * cosine, -weight * sine], axis=0)  14.2 us
    dot_general x1, matrix products, spectral_update(): jnp.einsum('fckr,fkq->fcrq', left, right, precision=highest)  14 us
    all_to_all x1, starting transfers between devices, all_by_exchange(): return jnp.concatenate(lax.all_to_all(sent, name, 0, 0), axis=d)  11.6 us
  transfers between devices with their start and end apart: 3, of which 2 were waited for; matrix products, arithmetic and copies ran while one was open for 13% of the time, Pallas kernels for 0%

profile of v1, /device:TPU:1, one launch (start us, length us, event | category | flops | bytes accessed | tf_op | source)
XLA Modules:
  0.0 288.4 jit_solution(9926440531719303541)
XLA Ops:
  0.7 3.1 %copy.50 = f32[2,32,16,384]{3,1,0,2:T(8,128)} copy(f32[2,32,16,384]{3,2,1,0:T(8,128)} %param.10) | data formatting | bytes 3145728 | tf_op args[0]
  3.8 7.6 %all-to-all-start = ((f32[2,32,16,384]{3,1,0,2:T(8,128)}), f32[2,32,16,384]{3,1,0,2:T(8,128)S(1)}, u32[]{:S(2)}, u32[]{:S(2)}) async-start(f32[2,32,16,384]{3,1,0,2:T(8,128)} %copy.50), calls=%async_computation | async-start | bytes 3145728 | tf_op jit(solution)/shard_map/all_to_all | solution.py:125
  11.6 14.2 %fusion.12 = (f32[512,1536]{1,0:T(8,128)}, f32[512,1536]{1,0:T(8,128)}) fusion(f32[512]{0:T(512)S(1)} %select_multiply_fusion, f32[512]{0:T(512)S(1)} %fusion.55), kind=kLoop, calls=%fused_computation.28 | loop fusion | flops 8650752 | bytes 6295552 | tf_op jit(solution)/shard_map/mul | solution.py:41
  25.8 14.3 %fusion.13 = (f32[512,1536]{1,0:T(8,128)}, f32[512,1536]{1,0:T(8,128)}) fusion(f32[512]{0:T(512)S(1)} %fusion.43, f32[512]{0:T(512)S(1)} %fusion.54), kind=kLoop, calls=%fused_computation.29 | loop fusion | flops 8650752 | bytes 6295552 | tf_op jit(solution)/shard_map/mul | solution.py:42
  42.1 12.0 %fusion.4 = f32[1536,384]{1,0:T(8,128)S(1)} fusion(f32[1024,384]{1,0:T(8,128)S(1)} %bitcast.90, f32[512,1536]{1,0:T(8,128)} %get-tuple-element.48, f32[512,1536]{1,0:T(8,128)S(1)} %copy-done.6), kind=kOutput, calls=%fused_computation.16 | convolution fusion | flops 7249920000 | bytes 10223616 | tf_op jit(solution)/shard_map/dot_general | solution.py:48
  54.1 10.1 %multiply_subtract_fusion.1 = f32[1024,384]{1,0:T(8,128)S(1)} fusion(f32[1024,384]{1,0:T(8,128)S(1)} %bitcast.91, f32[1536,384]{1,0:T(8,128)S(1)} %fusion.4, f32[512,1536]{1,0:T(8,128)S(1)} %copy-done.4, f32[512,1536]{1,0:T(8,128)S(1)} %copy-done.3), kind=kOutput, calls=%fused_computation.39 | convolution fusion | flops 7250116608 | bytes 11796480 | tf_op jit(solution)/shard_map/dot_general | solution.py:50
  64.3 3.2 %convolution_multiply_fusion = f32[2,512,384]{2,1,0:T(8,128)S(1)} fusion(f32[2,512,384]{2,1,0:T(8,128)S(1)} %bitcast.92, f32[512,384]{1,0:T(8,128)S(1)} %add_divide_fusion, f32[384,384]{1,0:T(8,128)S(1)} %copy-done), kind=kOutput, calls=%fused_computation.41 | convolution fusion | flops 1812332544 | bytes 4521984 | tf_op jit(solution)/shard_map/dot_general | solution.py:66
  67.5 3.4 %fusion.77 = f32[1024,384]{1,0:T(8,128)S(1)} fusion(f32[1024,384]{1,0:T(8,128)S(1)} %bitcast.88, f32[384,384]{1,0:T(8,128)S(1)} %copy-done.8), kind=kOutput, calls=%fused_computation.150 | convolution fusion | flops 1811939328 | bytes 3735552 | tf_op jit(solution)/shard_map/dot_general | solution.py:69
  71.0 10.0 %fusion.5 = f32[1536,384]{1,0:T(8,128)S(1)} fusion(f32[1024,384]{1,0:T(8,128)S(1)} %fusion.77, f32[512,1536]{1,0:T(8,128)S(1)} %copy-done.7, f32[512,1536]{1,0:T(8,128)S(1)} %copy-done.6), kind=kOutput, calls=%fused_computation.17 | convolution fusion | flops 7249920000 | bytes 10223616 | tf_op jit(solution)/shard_map/dot_general | solution.py:48
  81.0 10.1 %multiply_subtract_fusion = f32[1024,384]{1,0:T(8,128)S(1)} fusion(f32[1024,384]{1,0:T(8,128)S(1)} %fusion.77, f32[1536,384]{1,0:T(8,128)S(1)} %fusion.5, f32[512,1536]{1,0:T(8,128)S(1)} %copy-done.4, f32[512,1536]{1,0:T(8,128)S(1)} %copy-done.3), kind=kOutput, calls=%fused_computation.38 | convolution fusion | flops 7250116608 | bytes 11796480 | tf_op jit(solution)/shard_map/dot_general | solution.py:50
  91.1 3.2 %fusion.29 = f32[2,512,384]{2,1,0:T(8,128)S(1)} fusion(f32[2,512,384]{2,1,0:T(8,128)S(1)} %bitcast.89, f32[384,384]{1,0:T(8,128)S(1)} %copy-done), kind=kOutput, calls=%fused_computation.48 | convolution fusion | flops 1811939328 | bytes 3735552 | tf_op jit(solution)/shard_map/dot_general | solution.py:66
  94.3 3.3 %fusion.21 = f32[2,512,1,384]{3,1,0,2:T(8,128)S(1)} fusion(f32[2,512,384]{2,1,0:T(8,128)S(1)} %fusion.29, f32[512,384]{1,0:T(8,128)S(1)} %add_divide_fusion, f32[384,384]{1,0:T(8,128)S(1)} %copy-done.8), kind=kOutput, calls=%fused_computation.40 | convolution fusion | flops 1812332544 | bytes 4521984 | tf_op jit(solution)/shard_map/dot_general | solution.py:69
  97.7 3.7 %copy.52 = f32[4,512,1,384]{3,0,2,1:T(4,128)} copy(f32[4,512,1,384]{3,1,0,2:T(8,128)S(1)} %pad_maximum_fusion.10) | data formatting | bytes 6291456 | tf_op jit(solution)/shard_map/concatenate | solution.py:21
  101.4 6.8 %all-to-all-start.1 = ((f32[4,512,1,384]{3,0,2,1:T(4,128)}), f32[4,512,1,384]{3,0,2,1:T(4,128)}, u32[]{:S(2)}, u32[]{:S(2)}) async-start(f32[4,512,1,384]{3,0,2,1:T(4,128)} %copy.52), calls=%async_computation.1 | async-start | bytes 6291456 | tf_op jit(solution)/shard_map/all_to_all | solution.py:23
  114.9 33.6 %all-to-all-done.1 = f32[4,512,1,384]{3,0,2,1:T(4,128)} async-done(((f32[4,512,1,384]{3,0,2,1:T(4,128)}), f32[4,512,1,384]{3,0,2,1:T(4,128)}, u32[]{:S(2)}, u32[]{:S(2)}) %all-to-all-start.1) | async-done | bytes 3145760 | tf_op jit(solution)/shard_map/all_to_all | solution.py:23
  154.2 3.3 %pad_maximum_fusion.11 = f32[2,2,32,16,384]{4,1,3,2,0:T(2,128)} fusion(f32[1,2,32,16,384]{4,1,3,2,0:T(2,128)S(1)} %get-tuple-element.27, f32[1,2,32,16,384]{4,1,3,2,0:T(2,128)S(1)} %get-tuple-element.26), kind=kLoop, calls=%fused_computation.21 | loop fusion | flops 786432 | bytes 6291456 | tf_op jit(solution)/shard_map/stack | solution.py:143
  157.5 4.7 %gather_fusion.4 = f32[256,2,2,384]{3,2,1,0:T(2,128)S(1)} fusion(f32[2,2,32,16,384]{4,1,3,2,0:T(2,128)} %pad_maximum_fusion.11, s32[256]{0:T(256)S(1)} %bitcast.83), kind=kCustom, calls=%fused_computation.4 | custom fusion | bytes 3147776 | tf_op jit(solution)/shard_map/gather | solution.py:144
  163.1 3.5 %stack.26 = f32[128,2,2,8,384]{4,3,2,1,0:T(8,128)} broadcast(f32[2,2,8,384]{3,2,1,0:T(8,128)S(1)} %fusion.24), dimensions={1,2,3,4} | broadcast | bytes 6340608 | tf_op jit(solution)/shard_map/stack | solution.py:16
  166.6 11.6 %all-to-all-start.2 = ((f32[128,2,2,8,384]{4,3,2,1,0:T(8,128)}), f32[128,2,2,8,384]{4,3,2,1,0:T(8,128)}, u32[]{:S(2)}, u32[]{:S(2)}) async-start(f32[128,2,2,8,384]{4,3,2,1,0:T(8,128)} %stack.26), calls=%async_computation.2 | async-start | bytes 12582912 | tf_op jit(solution)/shard_map/all_to_all | solution.py:17
  181.8 71.6 %all-to-all-done.2 = f32[128,2,2,8,384]{4,3,2,1,0:T(8,128)} async-done(((f32[128,2,2,8,384]{4,3,2,1,0:T(8,128)}), f32[128,2,2,8,384]{4,3,2,1,0:T(8,128)}, u32[]{:S(2)}, u32[]{:S(2)}) %all-to-all-start.2) | async-done | bytes 6291488 | tf_op jit(solution)/shard_map/all_to_all | solution.py:17
  253.4 5.9 %copy.89 = f32[128,2,2,8,384]{4,3,0,2,1:T(8,128)} copy(f32[128,2,2,8,384]{4,3,2,1,0:T(8,128)} %all-to-all-done.2) | data formatting | bytes 12582912 | tf_op jit(solution)/shard_map/all_to_all | solution.py:17
  259.3 10.3 %copy.58 = f32[2,2,1024,384]{3,1,2,0:T(2,128)} copy(f32[2,2,1024,384]{3,2,1,0:T(8,128)} %bitcast.82) | data formatting | bytes 12582912 | tf_op jit(solution)/shard_map/reshape | solution.py:17
  269.6 3.4 %gather_fusion.5 = f32[2,2,2,384]{3,2,1,0:T(2,128)S(1)} fusion(f32[2,2,1024,384]{3,1,2,0:T(2,128)} %copy.58, s32[1024]{0:T(1024)S(1)} %pad_clamp_fusion), kind=kCustom, calls=%fused_computation.5 | custom fusion | bytes 24584 | tf_op jit(solution)/shard_map/jit(_take)/gather | solution.py:161
  273.9 14.0 %convolution_add_fusion = f32[2,4,2,384,384]{4,3,2,1,0:T(8,128)} fusion(f32[2,4,2,384,384]{4,3,2,1,0:T(8,128)} %param.19, f32[2,4,2,4,384]{4,1,3,0,2:T(4,128)S(1)} %pad_maximum_fusion.16, f32[2,4,4,384,1]{3,1,2,0,4:T(4,128)S(1)} %get-tuple-element.30), kind=kOutput, calls=%fused_computation.15 | convolution fusion | flops 115605504 | bytes 19021824 | tf_op jit(solution)/shard_map/vmap(fckr,fkq->fcrq)/dot_general | solution.py:100
  (69 shorter events, 19.1 us)
Async XLA Ops:
  0.6 63.7 %copy-start = (f32[384,384]{1,0:T(8,128)S(1)}, f32[384,384]{1,0:T(8,128)}, u32[]{:S(2)}) copy-start(f32[384,384]{1,0:T(8,128)} %param.12) | copy-start | bytes 1769476
  0.6 10.8 %copy-start.10 = (f32[384]{0:T(512)S(1)}, f32[384]{0:T(512)}, u32[]{:S(2)}) copy-start(f32[384]{0:T(512)} %param.13) | copy-start | bytes 4612
  3.8 36.4 %all-to-all-start = ((f32[2,32,16,384]{3,1,0,2:T(8,128)}), f32[2,32,16,384]{3,1,0,2:T(8,128)S(1)}, u32[]{:S(2)}, u32[]{:S(2)}) async-start(f32[2,32,16,384]{3,1,0,2:T(8,128)} %copy.50), calls=%async_computation | async-start | bytes 3145728 | tf_op jit(solution)/shard_map/all_to_all | solution.py:125
  40.2 1.9 copy-start.6
  42.1 12.0 %copy-start.3 = (f32[512,1536]{1,0:T(8,128)S(1)}, f32[512,1536]{1,0:T(8,128)}, u32[]{:S(2)}) copy-start(f32[512,1536]{1,0:T(8,128)} %get-tuple-element.49) | copy-start | bytes 9437188
  42.1 12.0 %copy-start.4 = (f32[512,1536]{1,0:T(8,128)S(1)}, f32[512,1536]{1,0:T(8,128)}, u32[]{:S(2)}) copy-start(f32[512,1536]{1,0:T(8,128)} %get-tuple-element.50) | copy-start | bytes 9437188
  64.3 3.2 %copy-start.8 = (f32[384,384]{1,0:T(8,128)S(1)}, f32[384,384]{1,0:T(8,128)}, u32[]{:S(2)}) copy-start(f32[384,384]{1,0:T(8,128)} %param.11) | copy-start | bytes 1769476
  64.3 6.7 %copy-start.7 = (f32[512,1536]{1,0:T(8,128)S(1)}, f32[512,1536]{1,0:T(8,128)}, u32[]{:S(2)}) copy-start(f32[512,1536]{1,0:T(8,128)} %get-tuple-element.48) | copy-start | bytes 9437188
  101.4 6.8 %copy-start.11 = (s32[256]{0:T(256)S(1)}, s32[256]{0:T(256)}, u32[]{:S(2)}) copy-start(s32[256]{0:T(256)} %param.15) | copy-start | bytes 3076
  101.4 8.3 %copy-start.2 = (s32[256,2]{0,1:T(2,128)S(1)}, s32[256,2]{0,1:T(2,128)}, u32[]{:S(2)}) copy-start(s32[256,2]{0,1:T(2,128)} %param.14) | copy-start | bytes 6148
  101.4 47.1 %all-to-all-start.1 = ((f32[4,512,1,384]{3,0,2,1:T(4,128)}), f32[4,512,1,384]{3,0,2,1:T(4,128)}, u32[]{:S(2)}, u32[]{:S(2)}) async-start(f32[4,512,1,384]{3,0,2,1:T(4,128)} %copy.52), calls=%async_computation.1 | async-start | bytes 6291456 | tf_op jit(solution)/shard_map/all_to_all | solution.py:23
  166.6 13.7 %copy-start.9 = (f32[2,4,2,384]{3,2,1,0:T(2,128)S(1)}, f32[2,4,2,384]{3,2,1,0:T(2,128)}, u32[]{:S(2)}) copy-start(f32[2,4,2,384]{3,2,1,0:T(2,128)} %param.18) | copy-start | bytes 73732
  166.6 13.8 %copy-start.12 = (s32[4]{0:T(128)S(1)}, s32[4]{0:T(128)}, u32[]{:S(2)}) copy-start(s32[4]{0:T(128)} %param.16) | copy-start | bytes 52
  166.6 13.9 %copy-start.5 = (f32[2,32,16,384]{3,0,2,1:T(2,128)S(1)}, f32[2,32,16,384]{3,0,2,1:T(2,128)}, u32[]{:S(2)}) copy-start(f32[2,32,16,384]{3,0,2,1:T(2,128)} %get-tuple-element.28) | copy-start | bytes 4718596
  166.6 86.9 %all-to-all-start.2 = ((f32[128,2,2,8,384]{4,3,2,1,0:T(8,128)}), f32[128,2,2,8,384]{4,3,2,1,0:T(8,128)}, u32[]{:S(2)}, u32[]{:S(2)}) async-start(f32[128,2,2,8,384]{4,3,2,1,0:T(8,128)} %stack.26), calls=%async_computation.2 | async-start | bytes 12582912 | tf_op jit(solution)/shard_map/all_to_all | solution.py:17
  273.9 14.0 %copy-start.1 = (f32[384,384]{1,0:T(8,128)S(1)}, f32[384,384]{1,0:T(8,128)}, u32[]{:S(2)}) copy-start(f32[384,384]{1,0:T(8,128)} %param.12) | copy-start | bytes 1769476
